TPU v7x, 256 devices: a whole 4x4x8 slice. The times are simulated.
256 devices in a mesh: req: 32 (over z, y), head: 8 (over x, core).
Axes of the slice: x: 4, y: 4, z: 8, core: 2. Of those that a mesh axis runs over, the one named last changes fastest.
Arguments:
- hidden: bfloat16 [512, 2048], P('req'), may hold values from -6 to 6
- deal_order: int32 [512], replicated, may hold values from 0 to 511, each once
- lengths: int32 [512], replicated, may hold values from 1 to 8192, as said below
- page_table: int32 [512, 64], replicated, may hold values from 0 to 2047, as said below
- key_cache: bfloat16 [2048, 128, 8, 128], P('req', None, 'head'), as said below
- value_cache: bfloat16 [2048, 128, 8, 128], P('req', None, 'head'), may hold values from -12 to 12
- attn_gain: float32 [2048], replicated, may hold values from 0.1 to 1.9
- w_query: bfloat16 [2048, 2048], P(None, 'head'), may hold values from -0.125 to 0.125
- w_key: bfloat16 [2048, 1024], P(None, 'head'), may hold values from -0.125 to 0.125
- w_value: bfloat16 [2048, 1024], P(None, 'head'), may hold values from -0.125 to 0.125
- w_gate: bfloat16 [2048, 2048], P(None, 'head'), may hold values from -0.125 to 0.125
- w_out: bfloat16 [2048, 2048], P('head'), may hold values from -1.5 to 1.5
- query_gain: float32 [128], replicated, may hold values from 0.5 to 2
- key_gain: float32 [128], replicated, may hold values from 0.5 to 2
- mlp_gain: float32 [2048], replicated, may hold values from 0.1 to 1.9
- mlp_gate: bfloat16 [2048, 3072], P(None, 'head'), may hold values from -0.125 to 0.125
- mlp_up: bfloat16 [2048, 3072], P(None, 'head'), may hold values from -0.125 to 0.125
- mlp_down: bfloat16 [3072, 2048], P('head'), may hold values from -0.109375 to 0.109375
Outputs:
- output: bfloat16 [512, 2048], P('req')
Inputs may be any that keep to these rules, and one draw needn't show every extreme that they name: `lengths`: one request holds exactly 8192 cached tokens, and all requests together fill at most 2048 pages of 128 tokens. `page_table`: for request r the first ceil(lengths[r] / 128) entries of row r name, in order, the pages that hold its cached tokens; no page is named by two such entries; the other entries are arbitrary page numbers. `key_cache`: cached keys; entries lie within -402 and 402.
All inputs are finite; a program needn't handle non-finite values.
Results may differ from a plain program's by a relative error of at most 0.022.
Values may be sent and summed in bfloat16 or wider, within the bound.
A program may use at most 64 MiB of HBM per device.

v0:
```python
import math
import jax
import jax.numpy as jnp
from jax import lax
from jax.sharding import PartitionSpec as P

EPSILON = 1e-06
ROPE_BASE = 1000000.0
LOW_SCORE = -1e30
LOG_TWO = math.log(2.0)


def rms_inv(values):
    return lax.rsqrt(jnp.mean(values * values, axis=-1, keepdims=True) + EPSILON)


def rotate(values, position):
    half_dim = values.shape[-1] // 2
    exponent = jnp.arange(half_dim, dtype=jnp.float32) * (2.0 / values.shape[-1])
    frequency = ROPE_BASE ** (-exponent)
    angles = position[:, None] * frequency[None, :]
    ones_tail = (1,) * (values.ndim - 2)
    angles = angles.reshape((angles.shape[0],) + ones_tail + (half_dim,))
    cosine = jnp.cos(angles)
    sine_vals = jnp.sin(angles)
    front_half = values[..., :half_dim]
    back_half = values[..., half_dim:]
    return jnp.concatenate(
        [front_half * cosine - back_half * sine_vals, back_half * cosine + front_half * sine_vals],
        axis=-1,
    )


def norm_rotate(values, gain_vec, position):
    return rotate(values * rms_inv(values) * gain_vec, position)


def pick_rows(wanted, shard_rows):
    targets = jnp.arange(shard_rows.shape[0], dtype=jnp.int32)
    selector = (wanted[:, None] == targets[None, :]).astype(jnp.bfloat16)
    return jnp.dot(selector, shard_rows, preferred_element_type=jnp.float32)


def body(
    hidden,
    deal_order,
    lengths,
    page_table,
    key_cache,
    value_cache,
    attn_gain,
    w_query,
    w_key,
    w_value,
    w_gate,
    w_out,
    query_gain,
    key_gain,
    mlp_gain,
    mlp_gate,
    mlp_up,
    mlp_down,
):
    local_rows, model_width = hidden.shape
    req_devices = lax.axis_size("req")
    req_index = lax.axis_index("req")
    all_rows = local_rows * req_devices
    head_width = query_gain.shape[0]
    pool_pages = key_cache.shape[0]
    page_size = key_cache.shape[1]
    local_kv = key_cache.shape[2]
    group_size = w_query.shape[1] // (local_kv * head_width)
    scale_factor = 1.0 / math.sqrt(head_width)
    first_own = req_index * local_rows
    hidden_f = hidden.astype(jnp.float32)
    normed = (hidden_f * rms_inv(hidden_f) * attn_gain).astype(jnp.bfloat16)
    own_requests = lax.dynamic_slice_in_dim(deal_order, first_own, local_rows)
    position = lengths[own_requests].astype(jnp.float32)
    queries = jnp.dot(normed, w_query, preferred_element_type=jnp.float32).reshape(
        local_rows, local_kv, group_size, head_width
    )
    queries = norm_rotate(queries, query_gain, position).astype(jnp.bfloat16)
    new_keys = jnp.dot(normed, w_key, preferred_element_type=jnp.float32).reshape(
        local_rows, local_kv, head_width
    )
    new_keys = norm_rotate(new_keys, key_gain, position).astype(jnp.bfloat16)
    new_values = (
        jnp.dot(normed, w_value, preferred_element_type=jnp.float32)
        .astype(jnp.bfloat16)
        .reshape(local_rows, local_kv, head_width)
    )
    gate_logits = jnp.dot(normed, w_gate, preferred_element_type=jnp.float32)
    all_queries = lax.all_gather(queries, "req", axis=0, tiled=True)
    dealt_lengths = lengths[deal_order]
    dealt_tables = page_table[deal_order]
    page_counts = (dealt_lengths + page_size - 1) // page_size
    slot_ids = jnp.arange(dealt_tables.shape[1], dtype=jnp.int32)
    local_ids = dealt_tables - req_index * pool_pages
    usable = (
        (slot_ids[None, :] < page_counts[:, None]) & (local_ids >= 0) & (local_ids < pool_pages)
    )
    targets = jnp.where(usable, local_ids, pool_pages).reshape(-1)
    request_ids = jnp.broadcast_to(
        jnp.arange(all_rows, dtype=jnp.int32)[:, None], dealt_tables.shape
    ).reshape(-1)
    slot_flat = jnp.broadcast_to(slot_ids[None, :], dealt_tables.shape).reshape(-1)
    owners = jnp.full((pool_pages,), all_rows, jnp.int32).at[targets].set(request_ids, mode="drop")
    owner_slots = jnp.zeros((pool_pages,), jnp.int32).at[targets].set(slot_flat, mode="drop")
    safe_owners = jnp.minimum(owners, all_rows - 1)
    filled = jnp.where(
        owners < all_rows,
        jnp.clip(dealt_lengths[safe_owners] - owner_slots * page_size, 0, page_size),
        0,
    )
    page_queries = all_queries[safe_owners]
    scores = (
        jnp.einsum("pkgd,ptkd->pkgt", page_queries, key_cache, preferred_element_type=jnp.float32)
        * scale_factor
    )
    live_mask = (
        jnp.arange(page_size, dtype=jnp.int32)[None, None, None, :] < filled[:, None, None, None]
    )
    scores = jnp.where(live_mask, scores, LOW_SCORE)
    page_peaks = jnp.max(scores, axis=-1)
    local_peaks = (
        jnp.full((all_rows, local_kv, group_size), LOW_SCORE, jnp.float32)
        .at[owners]
        .max(page_peaks, mode="drop")
    )
    self_scores = (
        jnp.einsum("rkgd,rkd->rkg", queries, new_keys, preferred_element_type=jnp.float32)
        * scale_factor
    )
    own_peaks = jnp.maximum(
        lax.dynamic_slice_in_dim(local_peaks, first_own, local_rows), self_scores
    )
    with_self = lax.dynamic_update_slice_in_dim(local_peaks, own_peaks, first_own, 0)
    global_peaks = lax.pmax(with_self, "req")
    global_shift = LOG_TWO * jnp.ceil(global_peaks / LOG_TWO)
    weights = jnp.where(live_mask, jnp.exp(scores - global_shift[safe_owners][..., None]), 0.0)
    totals = (
        jnp.zeros((all_rows, local_kv, group_size), jnp.float32)
        .at[owners]
        .add(jnp.sum(weights, axis=-1), mode="drop")
    )
    page_numerators = jnp.einsum(
        "pkgt,ptkd->pkgd",
        weights.astype(jnp.bfloat16),
        value_cache,
        preferred_element_type=jnp.float32,
    )
    numerators = (
        jnp.zeros((all_rows, local_kv, group_size, head_width), jnp.float32)
        .at[owners]
        .add(page_numerators, mode="drop")
    )
    totals, numerators = (totals, numerators)
    own_totals, own_numerators = (
        lax.psum_scatter(totals, "req", scatter_dimension=0, tiled=True),
        lax.psum_scatter(numerators, "req", scatter_dimension=0, tiled=True),
    )
    own_shift = lax.dynamic_slice_in_dim(global_shift, first_own, local_rows)
    self_weight = jnp.exp(self_scores - own_shift)
    own_totals = own_totals + self_weight
    self_rounded = lax.optimization_barrier(self_weight.astype(jnp.bfloat16)).astype(jnp.float32)
    own_numerators = (
        own_numerators + self_rounded[..., None] * new_values.astype(jnp.float32)[:, :, None, :]
    )
    heads_out = (own_numerators / own_totals[..., None]).reshape(
        local_rows, local_kv * group_size * head_width
    )
    attended = (heads_out * jax.nn.sigmoid(gate_logits)).astype(jnp.bfloat16)
    projected = jnp.dot(attended, w_out, preferred_element_type=jnp.float32)
    attn_total = lax.psum(projected.astype(jnp.bfloat16), "head").astype(jnp.float32)
    mixed_rows = (hidden_f + attn_total).astype(jnp.bfloat16)
    mixed_f = mixed_rows.astype(jnp.float32)
    normed_two = (mixed_f * rms_inv(mixed_f) * mlp_gain).astype(jnp.bfloat16)
    gate_part = jnp.dot(normed_two, mlp_gate, preferred_element_type=jnp.float32)
    up_part = jnp.dot(normed_two, mlp_up, preferred_element_type=jnp.float32)
    inner_act = (jax.nn.silu(gate_part) * up_part).astype(jnp.bfloat16)
    down_part = jnp.dot(inner_act, mlp_down, preferred_element_type=jnp.float32)
    inverse_order = (
        jnp.zeros((all_rows,), jnp.int32).at[deal_order].set(jnp.arange(all_rows, dtype=jnp.int32))
    )
    wanted = lax.dynamic_slice_in_dim(inverse_order, first_own, local_rows)
    mlp_total = lax.psum(down_part.astype(jnp.bfloat16), "head").astype(jnp.float32)
    result = (mixed_f + mlp_total).astype(jnp.bfloat16)
    gathered = pick_rows(wanted, lax.all_gather(result, "req", axis=0, tiled=True))
    output = gathered.astype(jnp.bfloat16)
    return output


def solution(mesh):
    return jax.shard_map(
        body,
        mesh=mesh,
        in_specs=(
            P("req", None),
            P(),
            P(),
            P(),
            P("req", None, "head", None),
            P("req", None, "head", None),
            P(),
            P(None, "head"),
            P(None, "head"),
            P(None, "head"),
            P(None, "head"),
            P("head", None),
            P(),
            P(),
            P(),
            P(None, "head"),
            P(None, "head"),
            P("head", None),
        ),
        out_specs=P("req", None),
        check_vma=False,
    )
```

profile of v0, /device:TPU:2, one launch (start us, length us, event | category | flops | bytes accessed | tf_op | source)
XLA Modules:
  0.0 1038.4 jit_solution(14262938876819041306)
XLA Ops:
  6.6 0.8 compare_select_fusion.1
  7.5 0.8 compare_select_fusion.2
  8.3 1.0 fusion.17
  9.3 3.6 gather_fusion
  12.9 0.7 gather_fusion.3
  13.6 0.3 fusion.77
  14.0 0.1 iota_compare_fusion
  14.2 0.1 lt.102
  14.3 0.1 multiply_cosine_fusion.1
  14.7 52.5 %all_gather.6 = bf16[512,1,2,128]{3,2,1,0:T(2,128)(2,1)S(1)} all-gather(bf16[16,1,2,128]{3,2,1,0:T(2,128)(2,1)S(1)} %pad_maximum_fusion), channel_id=1, replica_groups=mesh['req'=32,'head'=8] {'req'}, dimensions={0}, use_global_device_ids=true | all-gather | bytes 270336 | tf_op jit(solution)/shard_map/all_gather | solution.py:93
  67.2 0.1 copy.63
  67.3 1.0 gather_fusion.1
  68.4 0.2 sub.57
  68.9 0.4 compare_select_fusion
  69.3 120.0 %scatter_custom_fusion.2 = s32[64]{0:T(128)S(1)} fusion(s32[32768]{0:T(1024)S(1)} %bitcast.102, s32[32768]{0:T(1024)S(1)} %reshape.511, s32[]{:T(128)} %constant.24.clone.1), kind=kCustom, calls=%fused_computation.126 | custom fusion | bytes 260 | tf_op jit(solution)/shard_map/scatter | solution.py:108
  189.3 120.0 %scatter_custom_fusion.1 = s32[64]{0:T(128)S(1)} fusion(s32[32768]{0:T(1024)S(1)} %bitcast.103, s32[32768]{0:T(1024)S(1)} %reshape.503, s32[]{:T(128)} %constant.25.clone.1), kind=kCustom, calls=%fused_computation.128 | custom fusion | bytes 260 | tf_op jit(solution)/shard_map/scatter | solution.py:107
  309.4 0.8 gather_fusion.2
  310.2 0.6 gather_fusion.4
  310.9 1.3 fusion.80
  312.2 0.9 scatter_custom_fusion.3
  313.2 0.4 multiply_reduce_fusion.1
  313.7 0.1 fusion.56
  313.9 0.2 fusion.53
  314.2 0.1 dynamic_update_slice.3
  314.4 72.4 %pmax.7 = f32[512,1,2]{0,2,1:T(2,128)S(1)} all-reduce(f32[512,1,2]{0,2,1:T(2,128)S(1)} %dynamic_update_slice.3), channel_id=1, replica_groups=mesh['req'=32,'head'=8] {'req'}, use_global_device_ids=true, to_apply=%region_8.9 | all-reduce | flops 1024 | bytes 8192 | tf_op jit(solution)/shard_map/pmax | solution.py:138
  386.7 0.1 copy.68
  386.9 0.6 gather_fusion.5
  387.5 0.2 fusion.70
  387.7 1.5 scatter_custom_fusion.5
  389.3 2.3 fusion
  391.6 0.1 broadcast.362
  391.8 2.8 scatter_fusion
  394.6 0.8 copy.88
  395.5 0.2 fusion.16
  395.7 203.3 %reduce-scatter.10.cloned.1.call-done = f32[16,2]{1,0:T(8,128)} async-done(((f32[512,2]{1,0:T(8,128)}), f32[16,2]{1,0:T(8,128)}) %reduce-scatter.10.cloned.1.call-update) | async-done | bytes 144
  599.0 0.8 copy.77
  600.0 214.6 %reduce-scatter.8.cloned.1.call-done = f32[16,256]{1,0:T(8,128)} async-done(((f32[512,256]{1,0:T(8,128)}), f32[16,256]{1,0:T(8,128)}) %reduce-scatter.8.cloned.1.call-update) | async-done | bytes 16400
  814.7 0.7 reshape.564
  815.5 3.0 convolution_convert_fusion.2
  818.5 60.0 %all-reduce.3.cloned.1.call-done = bf16[16,2048]{1,0:T(8,128)(2,1)} async-done(((bf16[16,2048]{1,0:T(8,128)(2,1)}), bf16[16,2048]{1,0:T(8,128)(2,1)}) %all-reduce.3.cloned.1.call-update) | async-done | bytes 65552 | tf_op jit(solution)/shard_map/psum | solution.py:174
  878.5 1.0 fusion.21
  879.5 1.8 fusion.41
  881.3 3.3 convolution_convert_fusion.1
  884.7 62.9 %all-reduce.5.cloned.1.call-done = bf16[16,2048]{1,0:T(8,128)(2,1)} async-done(((bf16[16,2048]{1,0:T(8,128)(2,1)}), bf16[16,2048]{1,0:T(8,128)(2,1)}) %all-reduce.5.cloned.1.call-update) | async-done | bytes 65552 | tf_op jit(solution)/shard_map/psum | solution.py:186
  947.6 1.5 fusion.24
  949.1 2.4 scatter_custom_fusion
  951.6 77.6 %all-gather.2.cloned.1.call-done = bf16[512,2048]{1,0:T(8,128)(2,1)} async-done(((bf16[16,2048]{1,0:T(8,128)(2,1)}), bf16[512,2048]{1,0:T(8,128)(2,1)}) %all-gather.2.cloned.1.call-update) | async-done | bytes 2097168 | tf_op jit(solution)/shard_map/all_gather | solution.py:188
  1029.2 2.6 convolution_convert_fusion
  (70 shorter events, 2.0 us)
Async XLA Ops:
  6.5 304.4 %copy-start = (bf16[64,128,1,128]{3,1,2,0:T(8,128)(2,1)S(1)}, bf16[64,128,1,128]{3,1,2,0:T(8,128)(2,1)}, u32[]{:S(2)}) copy-start(bf16[64,128,1,128]{3,1,2,0:T(8,128)(2,1)} %param.22) | copy-start | bytes 6291460
  6.5 7.1 copy-start.2
  6.5 6.4 copy-start.1
  6.5 7.1 copy-start.6
  6.5 7.1 copy-start.3
  6.5 592.5 %reduce-scatter.10.cloned.1.call-start = ((), (), s32[]{:S(2)}) async-start(), calls=%async_computation.6 | async-start | bytes 270336
  9.2 5.2 copy-start.10
  12.9 54.3 %copy-start.7 = (s32[512,64]{0,1:T(8,128)S(1)}, s32[512,64]{0,1:T(8,128)}, u32[]{:S(2)}) copy-start(s32[512,64]{0,1:T(8,128)} %param.21) | copy-start | bytes 393220
  309.3 3.9 copy-start.4
  310.9 2.7 copy-start.9
  389.3 425.4 %reduce-scatter.8.cloned.1.call-start = ((), (), s32[]{:S(2)}) async-start(), calls=%async_computation.5 | async-start | bytes 540672
  391.6 3.9 copy-start.5
  395.4 484.1 %copy-start.8 = (f32[2048]{0:T(1024)S(1)}, f32[2048]{0:T(1024)}, u32[]{:S(2)}) copy-start(f32[2048]{0:T(1024)} %param.32) | copy-start | bytes 24580
  395.4 483.1 %all-reduce.3.cloned.1.call-start = ((), (), s32[]{:S(2)}) async-start(), calls=%async_computation.2 | async-start | bytes 131072 | tf_op jit(solution)/shard_map/psum | solution.py:174
  818.5 129.1 %all-reduce.5.cloned.1.call-start = ((), (), s32[]{:S(2)}) async-start(), calls=%async_computation.3 | async-start | bytes 131072 | tf_op jit(solution)/shard_map/psum | solution.py:186
  884.6 144.6 %all-gather.2.cloned.1.call-start = ((), (), s32[]{:S(2)}) async-start(), calls=%async_computation.4 | async-start | bytes 2162688 | tf_op jit(solution)/shard_map/all_gather | solution.py:188
Sparse Core Ops, SparseCore 0:
  389.4 209.5 reduce-scatter.9
  603.3 211.3 reduce-scatter.7
  818.6 59.8 all-reduce.2
  884.7 62.8 all-reduce.4
  950.0 79.1 all-gather.1
where the time goes:
time: 1040 us
  waiting for transfers between devices  619 us (60%)
  local copies, waits for them, and re-layouts  254 us (24%)
  blocking collectives  125 us (12%)
  matrix products  15.3 us (1%)
  between operations  13.5 us (1%)
  other arithmetic  12.2 us (1%)
    unnamed x7, waiting for transfers between devices  418 us
    scatter x1, local copies, waits for them, and re-layouts, body(): jnp.zeros((pool_pages,), jnp.int32).at[targets].set(slot_flat, mode='drop')  120 us
    scatter x1, local copies, waits for them, and re-layouts, body(): jnp.full((pool_pages,), all_rows, jnp.int32).at[targets]  120 us
    all_gather x1, waiting for transfers between devices, body(): lax.all_gather(result, 'req', axis=0, tiled=True)  77.6 us
    pmax x1, blocking collectives, body(): global_peaks = lax.pmax(with_self, 'req')  72.4 us
    psum x1, waiting for transfers between devices, body(): lax.psum(down_part.astype(jnp.bfloat16), 'head').astype(jnp.float32)  62.9 us
    psum x1, waiting for transfers between devices, body(): lax.psum(projected.astype(jnp.bfloat16), 'head').astype(jnp.float32)  60 us
    all_gather x1, blocking collectives, body(): all_queries = lax.all_gather(queries, 'req', axis=0, tiled=True)  52.5 us
  transfers between devices with their start and end apart: 5, of which 5 were waited for; matrix products, arithmetic and copies ran while one was open for 1% of the time, Pallas kernels for 0%

commit v1 on v0

--- a/solution.py
+++ b/solution.py
@@ -183,7 +183,9 @@
         jnp.zeros((all_rows,), jnp.int32).at[deal_order].set(jnp.arange(all_rows, dtype=jnp.int32))
     )
     wanted = lax.dynamic_slice_in_dim(inverse_order, first_own, local_rows)
-    mlp_total = lax.psum(down_part.astype(jnp.bfloat16), "head").astype(jnp.float32)
+    mlp_total = jnp.sum(lax.all_gather(down_part.astype(jnp.bfloat16), "head"), axis=0).astype(
+        jnp.float32
+    )
     result = (mixed_f + mlp_total).astype(jnp.bfloat16)
     gathered = pick_rows(wanted, lax.all_gather(result, "req", axis=0, tiled=True))
     output = gathered.astype(jnp.bfloat16)

time: 1040 us -> 988 us (0.950)
  waiting for transfers between devices: 619 us -> 556 us
  blocking collectives: 125 us -> 138 us
    psum x1 -> x0, waiting for transfers between devices: 62.9 us -> none  [body(): lax.psum(down_part.astype(jnp.bfloat16), 'head').astype(jnp.float32)]
    all_gather x0 -> x1, blocking collectives: none -> 13.1 us  [body(): lax.all_gather(down_part.astype(jnp.bfloat16), 'head')]
    unnamed x7 -> x6, waiting for transfers between devices: 418 us -> 418 us
  transfers between devices with their start and end apart: 5 -> 4, of which waited for: 5 -> 4; matrix products, arithmetic and copies ran while one was open for 1% -> 1% of each run, Pallas kernels for 0% -> 0%
where the time goes in v1:
time: 988 us; the launch traced here: 987 us
  waiting for transfers between devices  556 us (56%)
  local copies, waits for them, and re-layouts  254 us (26%)
  blocking collectives  138 us (14%)
  matrix products  14.7 us (1%)
  between operations  13.5 us (1%)
  other arithmetic  11.4 us (1%)
    unnamed x6, waiting for transfers between devices  418 us
    scatter x1, local copies, waits for them, and re-layouts, body(): jnp.zeros((pool_pages,), jnp.int32).at[targets].set(slot_flat, mode='drop')  120 us
    scatter x1, local copies, waits for them, and re-layouts, body(): jnp.full((pool_pages,), all_rows, jnp.int32).at[targets]  120 us
    all_gather x1, waiting for transfers between devices, body(): lax.all_gather(result, 'req', axis=0, tiled=True)  77.6 us
    pmax x1, blocking collectives, body(): global_peaks = lax.pmax(with_self, 'req')  72.4 us
    psum x1, waiting for transfers between devices, body(): lax.psum(projected.astype(jnp.bfloat16), 'head').astype(jnp.float32)  60 us
    all_gather x1, blocking collectives, body(): all_queries = lax.all_gather(queries, 'req', axis=0, tiled=True)  52.5 us
  transfers between devices with their start and end apart: 4, of which 4 were waited for; matrix products, arithmetic and copies ran while one was open for 1% of the time, Pallas kernels for 0%

profile of v1, /device:TPU:2, one launch (start us, length us, event | category | flops | bytes accessed | tf_op | source)
XLA Modules:
  0.0 987.1 jit_solution(17392821684033142270)
XLA Ops:
  6.6 0.8 compare_select_fusion.1
  7.5 0.8 compare_select_fusion.2
  8.3 1.0 fusion.17
  9.3 3.6 gather_fusion
  12.9 0.7 gather_fusion.3
  13.6 0.3 fusion.77
  14.0 0.1 iota_compare_fusion
  14.2 0.1 lt.102
  14.3 0.1 multiply_cosine_fusion.1
  14.7 52.5 %all_gather.12 = bf16[512,1,2,128]{3,2,1,0:T(2,128)(2,1)S(1)} all-gather(bf16[16,1,2,128]{3,2,1,0:T(2,128)(2,1)S(1)} %pad_maximum_fusion), channel_id=1, replica_groups=mesh['req'=32,'head'=8] {'req'}, dimensions={0}, use_global_device_ids=true | all-gather | bytes 270336 | tf_op jit(solution)/shard_map/all_gather | solution.py:93
  67.2 0.1 copy.63
  67.3 1.0 gather_fusion.1
  68.4 0.2 sub.57
  68.9 0.4 compare_select_fusion
  69.3 120.0 %scatter_custom_fusion.2 = s32[64]{0:T(128)S(1)} fusion(s32[32768]{0:T(1024)S(1)} %bitcast.104, s32[32768]{0:T(1024)S(1)} %reshape.511, s32[]{:T(128)} %constant.25.clone.1), kind=kCustom, calls=%fused_computation.126 | custom fusion | bytes 260 | tf_op jit(solution)/shard_map/scatter | solution.py:108
  189.3 120.0 %scatter_custom_fusion.1 = s32[64]{0:T(128)S(1)} fusion(s32[32768]{0:T(1024)S(1)} %bitcast.105, s32[32768]{0:T(1024)S(1)} %reshape.503, s32[]{:T(128)} %constant.26.clone.1), kind=kCustom, calls=%fused_computation.128 | custom fusion | bytes 260 | tf_op jit(solution)/shard_map/scatter | solution.py:107
  309.4 0.8 gather_fusion.2
  310.2 0.6 gather_fusion.4
  310.9 1.3 fusion.80
  312.2 0.9 scatter_custom_fusion.3
  313.2 0.4 multiply_reduce_fusion.1
  313.7 0.1 fusion.56
  313.9 0.2 fusion.53
  314.2 0.1 dynamic_update_slice.3
  314.4 72.4 %pmax.7 = f32[512,1,2]{0,2,1:T(2,128)S(1)} all-reduce(f32[512,1,2]{0,2,1:T(2,128)S(1)} %dynamic_update_slice.3), channel_id=1, replica_groups=mesh['req'=32,'head'=8] {'req'}, use_global_device_ids=true, to_apply=%region_8.9 | all-reduce | flops 1024 | bytes 8192 | tf_op jit(solution)/shard_map/pmax | solution.py:138
  386.7 0.1 copy.68
  386.9 0.6 gather_fusion.5
  387.5 0.2 fusion.70
  387.7 1.5 scatter_custom_fusion.5
  389.3 2.3 fusion
  391.6 0.1 broadcast.362
  391.8 2.8 scatter_fusion
  394.6 0.8 copy.88
  395.5 0.2 fusion.16
  395.7 203.3 %reduce-scatter.10.cloned.1.call-done = f32[16,2]{1,0:T(8,128)} async-done(((f32[512,2]{1,0:T(8,128)}), f32[16,2]{1,0:T(8,128)}) %reduce-scatter.10.cloned.1.call-update) | async-done | bytes 144
  599.0 0.8 copy.77
  600.0 214.6 %reduce-scatter.8.cloned.1.call-done = f32[16,256]{1,0:T(8,128)} async-done(((f32[512,256]{1,0:T(8,128)}), f32[16,256]{1,0:T(8,128)}) %reduce-scatter.8.cloned.1.call-update) | async-done | bytes 16400
  814.7 0.7 reshape.565
  815.5 3.0 convolution_convert_fusion.2
  818.5 60.0 %all-reduce.2.cloned.1.call-done = bf16[16,2048]{1,0:T(8,128)(2,1)} async-done(((bf16[16,2048]{1,0:T(8,128)(2,1)}), bf16[16,2048]{1,0:T(8,128)(2,1)}) %all-reduce.2.cloned.1.call-update) | async-done | bytes 65552 | tf_op jit(solution)/shard_map/psum | solution.py:174
  878.5 1.0 fusion.21
  879.5 1.8 fusion.41
  881.3 2.7 convolution_convert_fusion.1
  883.9 13.1 %all-gather = bf16[128,2048]{1,0:T(8,128)(2,1)S(1)} all-gather(bf16[16,2048]{1,0:T(8,128)(2,1)S(1)} %convolution_convert_fusion.1), channel_id=2, replica_groups=mesh['req'=32,'head'=8] {'head'}, dimensions={0}, use_global_device_ids=true | all-gather | bytes 589824 | tf_op jit(solution)/shard_map/all_gather | solution.py:186
  897.1 0.6 fusion.24
  897.8 2.4 scatter_custom_fusion
  900.3 77.6 %all-gather.3.cloned.1.call-done = bf16[512,2048]{1,0:T(8,128)(2,1)} async-done(((bf16[16,2048]{1,0:T(8,128)(2,1)}), bf16[512,2048]{1,0:T(8,128)(2,1)}) %all-gather.3.cloned.1.call-update) | async-done | bytes 2097168 | tf_op jit(solution)/shard_map/all_gather | solution.py:190
  977.9 2.6 convolution_convert_fusion
  (69 shorter events, 2.0 us)
Async XLA Ops:
  6.5 304.4 %copy-start = (bf16[64,128,1,128]{3,1,2,0:T(8,128)(2,1)S(1)}, bf16[64,128,1,128]{3,1,2,0:T(8,128)(2,1)}, u32[]{:S(2)}) copy-start(bf16[64,128,1,128]{3,1,2,0:T(8,128)(2,1)} %param.22) | copy-start | bytes 6291460
  6.5 7.1 copy-start.2
  6.5 6.4 copy-start.1
  6.5 7.1 copy-start.6
  6.5 7.1 copy-start.3
  6.5 592.5 %reduce-scatter.10.cloned.1.call-start = ((), (), s32[]{:S(2)}) async-start(), calls=%async_computation.5 | async-start | bytes 270336
  9.2 5.2 copy-start.10
  12.9 54.3 %copy-start.7 = (s32[512,64]{0,1:T(8,128)S(1)}, s32[512,64]{0,1:T(8,128)}, u32[]{:S(2)}) copy-start(s32[512,64]{0,1:T(8,128)} %param.21) | copy-start | bytes 393220
  309.3 3.9 copy-start.4
  310.9 2.7 copy-start.9
  389.3 425.4 %reduce-scatter.8.cloned.1.call-start = ((), (), s32[]{:S(2)}) async-start(), calls=%async_computation.4 | async-start | bytes 540672
  391.6 3.9 copy-start.5
  395.4 484.1 %copy-start.8 = (f32[2048]{0:T(1024)S(1)}, f32[2048]{0:T(1024)}, u32[]{:S(2)}) copy-start(f32[2048]{0:T(1024)} %param.32) | copy-start | bytes 24580
  395.4 483.1 %all-reduce.2.cloned.1.call-start = ((), (), s32[]{:S(2)}) async-start(), calls=%async_computation.2 | async-start | bytes 131072 | tf_op jit(solution)/shard_map/psum | solution.py:174
  818.5 159.4 %all-gather.3.cloned.1.call-start = ((), (), s32[]{:S(2)}) async-start(), calls=%async_computation.3 | async-start | bytes 2162688 | tf_op jit(solution)/shard_map/all_gather | solution.py:190
Sparse Core Ops, SparseCore 0:
  389.4 209.5 reduce-scatter.9
  603.3 211.3 reduce-scatter.7
  818.6 59.8 all-reduce.1
  897.9 79.9 all-gather.2
